TPU v7x, 256 devices: a whole 4x4x8 slice. The times are simulated.
256 devices in a mesh: rows: 64 (over x_hi, y, z), grp: 4 (over x_lo, core).
Axes of the slice: x: 4 (x_hi: 2, x_lo: 2; x = x_hi * 2 + x_lo), y: 4, z: 8, core: 2. Of those that a mesh axis runs over, the one named last changes fastest.
Arguments:
- table: float32 [524288, 256], P(('rows', 'grp')), may hold values from -1.5 to 1.5
- hot_slot: int32 [4096], P(('rows', 'grp')), may hold values from 0 to 2047, as said below
- cold_row: int32 [256, 256, 8], P(('rows', 'grp')), may hold values from 0 to 2047, as said below
- cold_bag: int32 [256, 256, 8], P(('rows', 'grp')), may hold values from 0 to 511
- hot_pick: int32 [65536, 8], P(('rows', 'grp')), may hold values from 0 to 4095
- dense: float32 [65536, 256], P(('rows', 'grp')), may hold values from -6 to 6
- label: int32 [65536], P(('rows', 'grp')), may hold values 0 or 1
Outputs:
- pooled: float32 [65536, 256], P(('rows', 'grp'))
- new_table: float32 [524288, 256], P(('rows', 'grp'))
- hot_new: float32 [4096, 256], replicated
Inputs may be any that keep to these rules, and one draw needn't show every extreme that they name: `hot_slot`: distinct within each device's block of 16 entries; hot row h lies in the shard of device h // 16. `cold_row`: a cold slot never names a hot row of its owner. `cold_bag`: a value of 256 or more marks an empty slot.
All inputs are finite; a program needn't handle non-finite values. No bound on the sum of `label` on one device may be relied on, other than what follows from the above.
Results may differ from a plain program's by a relative error of at most 0.0029.
Values may be sent and summed in bfloat16 or wider, within the bound.
A program may use at most 64 MiB of HBM per device.

v0:
```python
import jax
import jax.numpy as jnp
from jax import lax
from jax.sharding import PartitionSpec as P


def split_up(value, dim, peers):
    shape = value.shape
    blocks = value.reshape(*shape[:dim], peers, shape[dim] // peers, *shape[dim + 1 :])
    return jnp.moveaxis(blocks, dim, 0)


def laid_out(blocks, dim):
    blocks = jnp.moveaxis(blocks, 0, dim)
    shape = blocks.shape
    return blocks.reshape(*shape[:dim], shape[dim] * shape[dim + 1], *shape[dim + 2 :])


def exchange_both(value, axis, axes, splits, concats):
    sizes = [lax.axis_size(a) for a in axes]
    blocks = split_up(value, splits[0], sizes[0])
    blocks = jnp.moveaxis(split_up(blocks, splits[1] + 1, sizes[1]), 0, 1)
    inside = blocks.shape[2:]
    blocks = blocks.reshape(-1, *inside)
    blocks = lax.all_to_all(blocks, axis, split_axis=0, concat_axis=0, tiled=True)
    blocks = laid_out(blocks.reshape(*sizes, *inside), concats[0] + 1)
    return laid_out(blocks, concats[1])


def body(table, hot_slot, cold_row, cold_bag, hot_pick, dense, label):
    n_rows = lax.axis_size("rows")
    n_grp = lax.axis_size("grp")
    width = table.shape[1]
    samples = dense.shape[0]
    own_hot = hot_slot.shape[0]
    slots = cold_row.shape[1] * cold_row.shape[2]
    per_peer = cold_row.shape[2]
    rounded = table.astype(jnp.bfloat16)
    hot_full = lax.all_gather(table[hot_slot], ("rows", "grp"), axis=0, tiled=True)
    hot_copy = hot_full.astype(jnp.bfloat16)
    requests = cold_row[0].reshape(n_rows, n_grp, per_peer)
    arrived = exchange_both(requests, ("rows", "grp"), ("rows", "grp"), (0, 1), (0, 1))
    looked = rounded[arrived.reshape(-1)].reshape(n_rows, n_grp, per_peer, width)
    returned = lax.all_to_all(
        lax.all_to_all(looked, "rows", split_axis=0, concat_axis=0, tiled=True),
        "grp",
        split_axis=1,
        concat_axis=1,
        tiled=True,
    )
    flat_rows = returned.reshape(slots, width)
    bags = cold_bag[0].reshape(slots)
    selector = jnp.arange(samples, dtype=jnp.int32)[:, None] == bags[None, :]
    cold_pooled = jnp.dot(
        selector.astype(jnp.bfloat16), flat_rows, preferred_element_type=jnp.float32
    )
    hot_pooled = jnp.sum(hot_copy[hot_pick].astype(jnp.float32), axis=1)
    pooled = cold_pooled + hot_pooled
    score = jnp.sum(pooled * dense, axis=1) / width**0.5
    err = jax.nn.sigmoid(score) - label.astype(jnp.float32)
    grad = err[:, None] * dense
    slot_grad = lax.dot_general(
        selector.astype(jnp.float32),
        grad,
        (((0,), (0,)), ((), ())),
        precision=lax.Precision.HIGHEST,
        preferred_element_type=jnp.float32,
    )
    delivered = exchange_both(
        slot_grad.reshape(n_rows, n_grp, per_peer, width),
        ("rows", "grp"),
        ("rows", "grp"),
        (0, 1),
        (0, 1),
    )
    table_grad = jax.ops.segment_sum(
        delivered.reshape(slots, width), arrived.reshape(slots), num_segments=table.shape[0]
    )
    hot_total = hot_copy.shape[0]
    spread = jnp.repeat(grad, hot_pick.shape[1], axis=0)
    hot_local = jax.ops.segment_sum(spread, hot_pick.reshape(-1), num_segments=hot_total)
    summed = lax.psum(hot_local, ("rows", "grp"))
    start = lax.axis_index(("rows", "grp")) * own_hot
    own_grad = lax.dynamic_slice_in_dim(summed, start, own_hot, 0)
    table_grad = table_grad.at[hot_slot].add(own_grad)
    new_table = table - 0.1 * table_grad
    hot_new = hot_full - 0.1 * summed
    return (pooled, new_table, hot_new)


def solution(mesh):
    placed = (
        P(("rows", "grp"), None),
        P(("rows", "grp")),
        P(("rows", "grp"), None, None),
        P(("rows", "grp"), None, None),
        P(("rows", "grp"), None),
        P(("rows", "grp"), None),
        P(("rows", "grp")),
    )
    return jax.shard_map(
        body,
        mesh=mesh,
        in_specs=placed,
        out_specs=(P(("rows", "grp"), None), P(("rows", "grp"), None), P()),
        check_vma=False,
    )
```

profile of v0, /device:TPU:2, one launch (start us, length us, event | category | flops | bytes accessed | tf_op | source)
XLA Modules:
  0.0 783.1 jit_solution(3402326476514333365)
XLA Ops:
  7.2 0.7 compare_select_fusion.2
  7.9 0.5 copy-done.6
  8.4 2.8 gather_fusion.1
  11.2 1.5 copy.38
  12.7 14.7 %all-to-all-start = ((s32[256,1,1,8]{3,2,1,0:T(1,128)}), s32[256,1,1,8]{3,2,1,0:T(1,128)S(1)}, u32[]{:S(2)}, u32[]{:S(2)}) async-start(s32[256,1,1,8]{3,2,1,0:T(1,128)} %bitcast), calls=%async_computation | async-start | bytes 262144 | tf_op jit(solution)/shard_map/all_to_all | solution.py:25
  27.4 1.7 convert_element_type.14
  29.1 10.6 %all-to-all-done = s32[256,1,1,8]{3,2,1,0:T(1,128)S(1)} async-done(((s32[256,1,1,8]{3,2,1,0:T(1,128)}), s32[256,1,1,8]{3,2,1,0:T(1,128)S(1)}, u32[]{:S(2)}, u32[]{:S(2)}) %all-to-all-start) | async-done | bytes 8224 | tf_op jit(solution)/shard_map/all_to_all | solution.py:25
  39.6 0.2 reshape_reshape.6
  39.8 7.5 gather_fusion
  47.3 34.3 %all_to_all.20 = bf16[64,4,8,256]{3,2,1,0:T(8,128)(2,1)S(1)} all-to-all(bf16[64,4,8,256]{3,2,1,0:T(8,128)(2,1)S(1)} %bitcast.38), channel_id=1, replica_groups=mesh['rows'=64,'grp'=4] {'rows'}, dimensions={0} | all-to-all | bytes 2097152 | tf_op jit(solution)/shard_map/all_to_all | solution.py:45
  81.6 1.0 copy.39
  82.6 4.7 all-to-all-start.2
  87.3 0.8 copy.43
  88.7 12.2 %all-to-all-done.2 = bf16[64,4,8,256]{3,2,0,1:T(8,128)(2,1)S(1)} async-done(((bf16[64,4,8,256]{3,2,0,1:T(8,128)(2,1)}), bf16[64,4,8,256]{3,2,0,1:T(8,128)(2,1)S(1)}, u32[]{:S(2)}, u32[]{:S(2)}) %all-to-all-start.2) | async-done | bytes 1048608 | tf_op jit(solution)/shard_map/all_to_all | solution.py:44
  100.9 1.1 copy.40
  102.0 330.1 %all-gather.3.cloned.1.call-done = f32[4096,256]{1,0:T(8,128)} async-done(((f32[16,256]{1,0:T(8,128)}), f32[4096,256]{1,0:T(8,128)}) %all-gather.3.cloned.1.call-update) | async-done | bytes 4194320 | tf_op jit(solution)/shard_map/all_gather | solution.py:39
  432.1 2.4 convert_element_type.15
  434.5 7.5 gather_fusion.2
  442.0 0.7 convert_reduce_fusion
  442.7 0.1 copy.42
  442.9 2.0 multiply_reduce_fusion
  445.0 3.2 fusion.7
  448.2 9.4 %all-to-all-start.3 = ((f32[256,1,1,8,256]{4,3,2,1,0:T(8,128)}), f32[256,1,1,8,256]{4,3,2,1,0:T(8,128)S(1)}, u32[]{:S(2)}, u32[]{:S(2)}) async-start(f32[256,1,1,8,256]{4,3,2,1,0:T(8,128)} %fusion.7), calls=%async_computation.3 | async-start | bytes 4194304 | tf_op jit(solution)/shard_map/all_to_all | solution.py:25
  457.5 0.2 all-reduce.2.cloned.1.call-start
  458.0 13.8 %scatter_custom_fusion.1 = f32[4096,256]{1,0:T(8,128)} fusion(s32[2048]{0:T(1024)S(1)} %reshape.98, f32[]{:T(128)} %constant.15.clone.1, f32[256,256]{1,0:T(8,128)S(1)} %broadcast_multiply_fusion), kind=kCustom, calls=%fused_computation.10 | custom fusion | flops 524288 | bytes 4456452 | tf_op jit(solution)/shard_map/scatter-add | solution.py:81
  471.9 0.2 reshape.90
  472.0 0.8 copy.46
  472.9 277.2 %all-reduce.2.cloned.1.call-done = f32[4096,256]{1,0:T(8,128)} async-done(((f32[4096,256]{1,0:T(8,128)}), f32[4096,256]{1,0:T(8,128)}) %all-reduce.2.cloned.1.call-update) | async-done | bytes 4194320 | tf_op jit(solution)/shard_map/psum | solution.py:82
  750.1 6.0 multiply_subtract_fusion
  756.1 13.0 %scatter_custom_fusion = f32[2048,256]{1,0:T(8,128)} fusion(s32[2048]{0:T(1024)S(1)} %reshape.90, f32[256,1,1,8,256]{4,3,2,1,0:T(8,128)S(1)} %all-to-all-done.3, f32[]{:T(128)} %constant.15.clone.1), kind=kCustom, calls=%fused_computation.7 | custom fusion | flops 524288 | bytes 4194308 | tf_op jit(solution)/shard_map/scatter-add | solution.py:76
  769.2 3.9 scatter_custom_fusion.2
  773.0 3.2 multiply_subtract_fusion.1
  (30 shorter events, 0.9 us)
Async XLA Ops:
  7.2 425.0 %all-gather.3.cloned.1.call-start = ((), (), s32[]{:S(2)}) async-start(), calls=%async_computation.5 | async-start | bytes 4210688 | tf_op jit(solution)/shard_map/all_gather | solution.py:39
  7.9 0.5 copy-start.6
  12.7 27.0 %all-to-all-start = ((s32[256,1,1,8]{3,2,1,0:T(1,128)}), s32[256,1,1,8]{3,2,1,0:T(1,128)S(1)}, u32[]{:S(2)}, u32[]{:S(2)}) async-start(s32[256,1,1,8]{3,2,1,0:T(1,128)} %bitcast), calls=%async_computation | async-start | bytes 262144 | tf_op jit(solution)/shard_map/all_to_all | solution.py:25
  81.6 5.7 copy-start.1
  81.6 6.6 copy-start.2
  81.6 6.8 copy-start.4
  82.6 18.3 %all-to-all-start.2 = ((bf16[64,4,8,256]{3,2,0,1:T(8,128)(2,1)}), bf16[64,4,8,256]{3,2,0,1:T(8,128)(2,1)S(1)}, u32[]{:S(2)}, u32[]{:S(2)}) async-start(bf16[64,4,8,256]{3,2,0,1:T(8,128)(2,1)} %copy.39), calls=%async_computation.2 | async-start | bytes 2097152 | tf_op jit(solution)/shard_map/all_to_all | solution.py:44
  442.0 2.8 copy-start.5
  448.2 9.6 %copy-start.3 = (s32[256,8]{0,1:T(8,128)S(1)}, s32[256,8]{0,1:T(8,128)}, u32[]{:S(2)}) copy-start(s32[256,8]{0,1:T(8,128)} %param.11) | copy-start | bytes 24580
  448.2 308.0 %all-to-all-start.3 = ((f32[256,1,1,8,256]{4,3,2,1,0:T(8,128)}), f32[256,1,1,8,256]{4,3,2,1,0:T(8,128)S(1)}, u32[]{:S(2)}, u32[]{:S(2)}) async-start(f32[256,1,1,8,256]{4,3,2,1,0:T(8,128)} %fusion.7), calls=%async_computation.3 | async-start | bytes 4194304 | tf_op jit(solution)/shard_map/all_to_all | solution.py:25
  457.5 292.6 %all-reduce.2.cloned.1.call-start = ((), (), s32[]{:S(2)}) async-start(), calls=%async_computation.4 | async-start | bytes 8388608 | tf_op jit(solution)/shard_map/psum | solution.py:82
  769.2 3.9 copy-start
Sparse Core Ops, SparseCore 0:
  11.3 420.7 all-gather.2
  472.0 278.0 all-reduce.1
where the time goes:
time: 784 us; the launch traced here: 783 us
  waiting for transfers between devices  630 us (80%)
  other arithmetic  45.5 us (6%)
  blocking collectives  34.3 us (4%)
  starting transfers between devices  29 us (4%)
  local copies, waits for them, and re-layouts  24.8 us (3%)
  between operations  14.2 us (2%)
    all_gather x1, waiting for transfers between devices, body(): lax.all_gather(table[hot_slot], ('rows', 'grp'), axis=0, tiled=True)  330 us
    psum x1, waiting for transfers between devices, body(): summed = lax.psum(hot_local, ('rows', 'grp'))  277 us
    all_to_all x1, blocking collectives, body(): lax.all_to_all(looked, 'rows', split_axis=0, concat_axis=0, tiled=True)  34.3 us
    all_to_all x2, starting transfers between devices, exchange_both(): lax.all_to_all(blocks, axis, split_axis=0, concat_axis=0, tiled=True)  24 us
  transfers between devices with their start and end apart: 5, of which 4 were waited for; matrix products, arithmetic and copies ran while one was open for 5% of the time, Pallas kernels for 0%

commit v1 on v0

--- a/solution.py
+++ b/solution.py
@@ -2,6 +2,7 @@
 import jax.numpy as jnp
 from jax import lax
 from jax.sharding import PartitionSpec as P
+from jax.lax import psum
 
 
 def split_up(value, dim, peers):
@@ -79,7 +80,7 @@
     hot_total = hot_copy.shape[0]
     spread = jnp.repeat(grad, hot_pick.shape[1], axis=0)
     hot_local = jax.ops.segment_sum(spread, hot_pick.reshape(-1), num_segments=hot_total)
-    summed = lax.psum(hot_local, ("rows", "grp"))
+    summed = psum(psum(hot_local, axis_name="rows"), axis_name="grp")
     start = lax.axis_index(("rows", "grp")) * own_hot
     own_grad = lax.dynamic_slice_in_dim(summed, start, own_hot, 0)
     table_grad = table_grad.at[hot_slot].add(own_grad)

time: 784 us -> 1300 us (1.66)
  waiting for transfers between devices: 630 us -> 1150 us
    psum x1 -> x2, waiting for transfers between devices: 277 us -> 746 us  [body(): summed = psum(psum(hot_local, axis_name='rows'), axis_name='grp')]
    all_to_all x2, waiting for transfers between devices: 10.6 us -> 61.2 us  [exchange_both(): lax.all_to_all(blocks, axis, split_axis=0, concat_axis=0, tiled=True)]
  transfers between devices with their start and end apart: 5 -> 6, of which waited for: 4 -> 6; matrix products, arithmetic and copies ran while one was open for 5% -> 2% of each run, Pallas kernels for 0% -> 0%
where the time goes in v1:
time: 1300 us
  waiting for transfers between devices  1150 us (88%)
  other arithmetic  44.4 us (3%)
  blocking collectives  34.3 us (3%)
  starting transfers between devices  29.3 us (2%)
  local copies, waits for them, and re-layouts  25.4 us (2%)
  between operations  13.9 us (1%)
    psum x2, waiting for transfers between devices, body(): summed = psum(psum(hot_local, axis_name='rows'), axis_name='grp')  746 us
    all_gather x1, waiting for transfers between devices, body(): lax.all_gather(table[hot_slot], ('rows', 'grp'), axis=0, tiled=True)  330 us
    all_to_all x2, waiting for transfers between devices, exchange_both(): lax.all_to_all(blocks, axis, split_axis=0, concat_axis=0, tiled=True)  61.2 us
    all_to_all x1, blocking collectives, body(): lax.all_to_all(looked, 'rows', split_axis=0, concat_axis=0, tiled=True)  34.3 us
  transfers between devices with their start and end apart: 6, of which 6 were waited for; matrix products, arithmetic and copies ran while one was open for 2% of the time, Pallas kernels for 0%

profile of v1, /device:TPU:2, one launch (start us, length us, event | category | flops | bytes accessed | tf_op | source)
XLA Modules:
  0.0 1301.0 jit_solution(3285122793624901062)
XLA Ops:
  7.2 0.7 compare_select_fusion.2
  7.9 0.6 copy-done.6
  8.5 2.8 gather_fusion.1
  11.2 1.5 copy.38
  12.7 14.7 %all-to-all-start = ((s32[256,1,1,8]{3,2,1,0:T(1,128)}), s32[256,1,1,8]{3,2,1,0:T(1,128)S(1)}, u32[]{:S(2)}, u32[]{:S(2)}) async-start(s32[256,1,1,8]{3,2,1,0:T(1,128)} %bitcast), calls=%async_computation | async-start | bytes 262144 | tf_op jit(solution)/shard_map/all_to_all | solution.py:26
  27.4 1.7 convert_element_type.14
  29.1 10.6 all-to-all-done
  39.7 0.2 reshape_reshape.6
  39.9 7.5 gather_fusion
  47.4 34.3 %all_to_all.20 = bf16[64,4,8,256]{3,2,1,0:T(8,128)(2,1)S(1)} all-to-all(bf16[64,4,8,256]{3,2,1,0:T(8,128)(2,1)S(1)} %bitcast.38), channel_id=1, replica_groups=mesh['rows'=64,'grp'=4] {'rows'}, dimensions={0} | all-to-all | bytes 2097152 | tf_op jit(solution)/shard_map/all_to_all | solution.py:46
  81.7 1.0 copy.39
  82.7 4.7 all-to-all-start.2
  87.4 0.8 copy.43
  88.9 0.7 reshape.98
  89.6 11.4 all-to-all-done.2
  101.0 1.1 copy.40
  102.1 330.1 %all-gather.3.cloned.1.call-done = f32[4096,256]{1,0:T(8,128)} async-done(((f32[16,256]{1,0:T(8,128)}), f32[4096,256]{1,0:T(8,128)}) %all-gather.3.cloned.1.call-update) | async-done | bytes 4194320 | tf_op jit(solution)/shard_map/all_gather | solution.py:40
  432.2 2.4 convert_element_type.15
  434.6 7.5 gather_fusion.2
  442.1 0.7 convert_reduce_fusion
  443.0 2.0 multiply_reduce_fusion
  445.1 14.0 %scatter_custom_fusion.1 = f32[4096,256]{1,0:T(8,128)} fusion(s32[2048]{0:T(1024)} %reshape.98, f32[]{:T(128)} %constant.15.clone.1, f32[256,256]{1,0:T(8,128)S(1)} %broadcast_multiply_fusion), kind=kCustom, calls=%fused_computation.10 | custom fusion | flops 524288 | bytes 4456960 | tf_op jit(solution)/shard_map/scatter-add | solution.py:82
  459.1 705.5 %all-reduce.3.cloned.1.call-done = f32[4096,256]{1,0:T(8,128)} async-done(((f32[4096,256]{1,0:T(8,128)}), f32[4096,256]{1,0:T(8,128)}) %all-reduce.3.cloned.1.call-update) | async-done | bytes 4194320 | tf_op jit(solution)/shard_map/psum | solution.py:83
  1164.7 3.2 fusion.7
  1167.9 9.8 all-to-all-start.3
  1177.8 0.8 copy.46
  1178.7 50.6 %all-to-all-done.3 = f32[256,1,1,8,256]{4,3,2,1,0:T(8,128)S(1)} async-done(((f32[256,1,1,8,256]{4,3,2,1,0:T(8,128)}), f32[256,1,1,8,256]{4,3,2,1,0:T(8,128)S(1)}, u32[]{:S(2)}, u32[]{:S(2)}) %all-to-all-start.3) | async-done | bytes 2097184 | tf_op jit(solution)/shard_map/all_to_all | solution.py:26
  1229.3 13.0 %scatter_custom_fusion = f32[2048,256]{1,0:T(8,128)} fusion(s32[2048]{0:T(1024)S(1)} %reshape.90, f32[256,1,1,8,256]{4,3,2,1,0:T(8,128)S(1)} %all-to-all-done.3, f32[]{:T(128)} %constant.15.clone.1), kind=kCustom, calls=%fused_computation.7 | custom fusion | flops 524288 | bytes 4194308 | tf_op jit(solution)/shard_map/scatter-add | solution.py:77
  1242.3 40.4 %all-reduce.5.cloned.1.call-done = f32[4096,256]{1,0:T(8,128)} async-done(((f32[4096,256]{1,0:T(8,128)}), f32[4096,256]{1,0:T(8,128)}) %all-reduce.5.cloned.1.call-update) | async-done | bytes 4194320 | tf_op jit(solution)/shard_map/psum | solution.py:83
  1282.7 3.7 scatter_custom_fusion.2
  1286.4 3.3 multiply_subtract_fusion.1
  1289.7 4.7 multiply_subtract_fusion
  (33 shorter events, 1.2 us)
Async XLA Ops:
  7.2 425.1 %all-gather.3.cloned.1.call-start = ((), (), s32[]{:S(2)}) async-start(), calls=%async_computation.6 | async-start | bytes 4210688 | tf_op jit(solution)/shard_map/all_gather | solution.py:40
  7.9 0.6 copy-start.6
  12.7 27.0 %all-to-all-start = ((s32[256,1,1,8]{3,2,1,0:T(1,128)}), s32[256,1,1,8]{3,2,1,0:T(1,128)S(1)}, u32[]{:S(2)}, u32[]{:S(2)}) async-start(s32[256,1,1,8]{3,2,1,0:T(1,128)} %bitcast), calls=%async_computation | async-start | bytes 262144 | tf_op jit(solution)/shard_map/all_to_all | solution.py:26
  81.7 5.8 copy-start.2
  81.7 6.6 copy-start.3
  81.7 7.0 copy-start.4
  82.7 18.3 %all-to-all-start.2 = ((bf16[64,4,8,256]{3,2,0,1:T(8,128)(2,1)}), bf16[64,4,8,256]{3,2,0,1:T(8,128)(2,1)S(1)}, u32[]{:S(2)}, u32[]{:S(2)}) async-start(bf16[64,4,8,256]{3,2,0,1:T(8,128)(2,1)} %copy.39), calls=%async_computation.2 | async-start | bytes 2097152 | tf_op jit(solution)/shard_map/all_to_all | solution.py:45
  87.4 1077.3 %all-reduce.3.cloned.1.call-start = ((), (), s32[]{:S(2)}) async-start(), calls=%async_computation.4 | async-start | bytes 8388608 | tf_op jit(solution)/shard_map/psum | solution.py:83
  442.1 2.8 copy-start.5
  459.1 823.6 %all-reduce.5.cloned.1.call-start = ((), (), s32[]{:S(2)}) async-start(), calls=%async_computation.5 | async-start | bytes 8388608 | tf_op jit(solution)/shard_map/psum | solution.py:83
  1167.9 61.4 %all-to-all-start.3 = ((f32[256,1,1,8,256]{4,3,2,1,0:T(8,128)}), f32[256,1,1,8,256]{4,3,2,1,0:T(8,128)S(1)}, u32[]{:S(2)}, u32[]{:S(2)}) async-start(f32[256,1,1,8,256]{4,3,2,1,0:T(8,128)} %fusion.7), calls=%async_computation.3 | async-start | bytes 4194304 | tf_op jit(solution)/shard_map/all_to_all | solution.py:26
  1242.3 44.1 %copy-start.1 = (f32[2048,256]{1,0:T(8,128)S(1)}, f32[2048,256]{1,0:T(8,128)}, u32[]{:S(2)}) copy-start(f32[2048,256]{1,0:T(8,128)} %param.7) | copy-start | bytes 6291460
  1286.4 3.3 copy-start
Sparse Core Ops, SparseCore 0:
  11.4 420.8 all-gather.2
  459.2 705.4 all-reduce.2
  1167.4 115.2 all-reduce.4
